TPU v7x, 32 devices: a whole 2x2x4 slice. The times are simulated.
32 devices in a mesh: seq: 2 (over x), fsdp: 16 (over z, y, core).
Axes of the slice: x: 2, y: 2, z: 4, core: 2. Of those that a mesh axis runs over, the one named last changes fastest.
Arguments:
- frames_in: float32 [16, 256, 768], P('fsdp', 'seq'), may hold values from -6 to 6
- cotangent: float32 [16, 256, 768], P('fsdp', 'seq'), may hold values from -6 to 6
- first_gain: bfloat16 [1, 768], P(None, 'fsdp'), may hold values from 0.099609375 to 1.8984375
- first_bias: bfloat16 [1, 768], P(None, 'fsdp'), may hold values from -3 to 3
- query_weight: bfloat16 [1, 768, 768], P(None, 'fsdp'), may hold values from -0.21875 to 0.21875
- query_bias: bfloat16 [1, 768], P(None, 'fsdp'), may hold values from -3 to 3
- key_weight: bfloat16 [1, 768, 768], P(None, 'fsdp'), may hold values from -0.21875 to 0.21875
- value_weight: bfloat16 [1, 768, 768], P(None, 'fsdp'), may hold values from -0.21875 to 0.21875
- value_bias: bfloat16 [1, 768], P(None, 'fsdp'), may hold values from -3 to 3
- out_weight: bfloat16 [1, 768, 768], P(None, 'fsdp'), may hold values from -3.5 to 3.5
- out_bias: bfloat16 [1, 768], P(None, 'fsdp'), may hold values from -3 to 3
- second_gain: bfloat16 [1, 768], P(None, 'fsdp'), may hold values from 0.099609375 to 1.8984375
- second_bias: bfloat16 [1, 768], P(None, 'fsdp'), may hold values from -3 to 3
- up_weight: bfloat16 [1, 768, 3072], P(None, 'fsdp'), may hold values from -0.21875 to 0.21875
- up_bias: bfloat16 [1, 3072], P(None, 'fsdp'), may hold values from -3 to 3
- down_weight: bfloat16 [1, 3072, 768], P(None, 'fsdp'), may hold values from -0.109375 to 0.109375
- down_bias: bfloat16 [1, 768], P(None, 'fsdp'), may hold values from -3 to 3
Outputs:
- outputs: float32 [16, 256, 768], P('fsdp', 'seq')
- input_gradient: float32 [16, 256, 768], P('fsdp', 'seq')
- first_gain_gradient: float32 [1, 768], P(None, 'fsdp')
- first_bias_gradient: float32 [1, 768], P(None, 'fsdp')
- query_weight_gradient: float32 [1, 768, 768], P(None, 'fsdp')
- query_bias_gradient: float32 [1, 768], P(None, 'fsdp')
- key_weight_gradient: float32 [1, 768, 768], P(None, 'fsdp')
- value_weight_gradient: float32 [1, 768, 768], P(None, 'fsdp')
- value_bias_gradient: float32 [1, 768], P(None, 'fsdp')
- out_weight_gradient: float32 [1, 768, 768], P(None, 'fsdp')
- out_bias_gradient: float32 [1, 768], P(None, 'fsdp')
- second_gain_gradient: float32 [1, 768], P(None, 'fsdp')
- second_bias_gradient: float32 [1, 768], P(None, 'fsdp')
- up_weight_gradient: float32 [1, 768, 3072], P(None, 'fsdp')
- up_bias_gradient: float32 [1, 3072], P(None, 'fsdp')
- down_weight_gradient: float32 [1, 3072, 768], P(None, 'fsdp')
- down_bias_gradient: float32 [1, 768], P(None, 'fsdp')
All inputs are finite; a program needn't handle non-finite values.
Results may differ from a plain program's by a relative error of at most 0.012.
The roundings to bfloat16 on the way count: a program that leaves them out, or rounds other values in their place, can miss the bound.
Values may be sent and summed in bfloat16 or wider, within the bound.
A program may use at most 128 MiB of HBM per device.

v0:
```python
import jax
import jax.numpy as jnp
from jax import lax
from jax.sharding import PartitionSpec as P

HEAD_DIM = 64
EPSILON = 1e-05
ROOT_HALF = 0.7071067811865476
INV_ROOT_TAU = 0.3989422804014327


def matmul(left, right):
    return jnp.dot(left, right, preferred_element_type=jnp.float32)


def contract_rows(left, right):
    return lax.dot_general(
        left, right, (((0,), (0,)), ((), ())), preferred_element_type=jnp.float32
    )


def contract_cols(left, right):
    return lax.dot_general(
        left, right, (((1,), (1,)), ((), ())), preferred_element_type=jnp.float32
    )


def layer_norm(residual, gain, offset):
    centre = residual - jnp.mean(residual, axis=-1, keepdims=True)
    inv_std = lax.rsqrt(jnp.mean(centre * centre, axis=-1, keepdims=True) + EPSILON)
    normed = centre * inv_std
    return (normed * gain.astype(jnp.float32) + offset.astype(jnp.float32), normed, inv_std)


def norm_grad(upstream, normed, inv_std, gain):
    scaled = upstream * gain.astype(jnp.float32)
    spread = scaled - jnp.mean(scaled, axis=-1, keepdims=True)
    return (spread - normed * jnp.mean(scaled * normed, axis=-1, keepdims=True)) * inv_std


def gelu_exact(pre_act):
    return 0.5 * pre_act * (1.0 + lax.erf(pre_act * ROOT_HALF))


def gelu_slope(pre_act):
    return (
        0.5 * (1.0 + lax.erf(pre_act * ROOT_HALF))
        + pre_act * jnp.exp(-0.5 * pre_act * pre_act) * INV_ROOT_TAU
    )


def split_heads(rows):
    return rows.reshape(rows.shape[0], rows.shape[1] // HEAD_DIM, HEAD_DIM)


def attend(query_rows, key_rows, value_rows):
    score_scale = HEAD_DIM ** (-0.5)
    query_heads = split_heads(query_rows)
    key_heads = split_heads(key_rows)
    value_heads = split_heads(value_rows)
    scores = (
        jnp.einsum("qhd,khd->hqk", query_heads, key_heads, preferred_element_type=jnp.float32)
        * score_scale
    )
    row_top = jnp.max(scores, axis=-1, keepdims=True)
    log_total = row_top + jnp.log(jnp.sum(jnp.exp(scores - row_top), axis=-1, keepdims=True))
    weights_low = jnp.exp(scores - log_total).astype(jnp.bfloat16)
    context = jnp.einsum(
        "hqk,khd->qhd", weights_low, value_heads, preferred_element_type=jnp.float32
    )
    return (context.reshape(query_rows.shape).astype(jnp.bfloat16), log_total)


def attend_back(query_rows, key_rows, value_rows, log_total, context_gradient):
    score_scale = HEAD_DIM ** (-0.5)
    row_shape = query_rows.shape
    query_heads = split_heads(query_rows)
    key_heads = split_heads(key_rows)
    value_heads = split_heads(value_rows)
    gradient_heads = split_heads(context_gradient)
    scores = (
        jnp.einsum("qhd,khd->hqk", query_heads, key_heads, preferred_element_type=jnp.float32)
        * score_scale
    )
    weights = jnp.exp(scores - log_total)
    weights_low = weights.astype(jnp.bfloat16)
    value_gradient = jnp.einsum(
        "hqk,qhd->khd", weights_low, gradient_heads, preferred_element_type=jnp.float32
    )
    prob_gradient = jnp.einsum(
        "qhd,khd->hqk", gradient_heads, value_heads, preferred_element_type=jnp.float32
    )
    score_gradient = (
        weights
        * (prob_gradient - jnp.sum(weights * prob_gradient, axis=-1, keepdims=True))
        * score_scale
    ).astype(jnp.bfloat16)
    query_gradient = jnp.einsum(
        "hqk,khd->qhd", score_gradient, key_heads, preferred_element_type=jnp.float32
    )
    key_gradient = jnp.einsum(
        "hqk,qhd->khd", score_gradient, query_heads, preferred_element_type=jnp.float32
    )
    return jnp.stack(
        [
            query_gradient.reshape(row_shape),
            key_gradient.reshape(row_shape),
            value_gradient.reshape(row_shape),
        ]
    ).astype(jnp.bfloat16)


def gather_layer(shards):
    return (
        lax.all_gather(shards[0], "fsdp", axis=0, tiled=True),
        lax.all_gather(shards[1], "fsdp", axis=0, tiled=True),
        lax.all_gather(shards[2], "fsdp", axis=0, tiled=True),
        lax.all_gather(shards[3], "fsdp", axis=0, tiled=True),
        lax.all_gather(shards[4], "fsdp", axis=0, tiled=True),
        lax.all_gather(shards[5], "fsdp", axis=0, tiled=True),
        lax.all_gather(shards[6], "fsdp", axis=0, tiled=True),
        lax.all_gather(shards[7], "fsdp", axis=0, tiled=True),
        lax.all_gather(shards[8], "fsdp", axis=0, tiled=True),
        lax.all_gather(shards[9], "fsdp", axis=0, tiled=True),
        lax.all_gather(shards[10], "fsdp", axis=0, tiled=True),
        lax.all_gather(shards[11], "fsdp", axis=0, tiled=True),
        lax.all_gather(shards[12], "fsdp", axis=0, tiled=True),
        lax.all_gather(shards[13], "fsdp", axis=0, tiled=True),
        lax.all_gather(shards[14], "fsdp", axis=0, tiled=True),
    )


def forward_layer(residual, params):
    hidden_wide, normed_in, inv_in = layer_norm(residual, params[0], params[1])
    hidden = hidden_wide.astype(jnp.bfloat16)
    query_rows = (matmul(hidden, params[2]) + params[3].astype(jnp.float32)).astype(jnp.bfloat16)
    key_rows = matmul(hidden, params[4]).astype(jnp.bfloat16)
    value_rows = (matmul(hidden, params[5]) + params[6].astype(jnp.float32)).astype(jnp.bfloat16)
    by_head = lax.all_to_all(
        jnp.stack([query_rows, key_rows, value_rows]),
        "seq",
        split_axis=2,
        concat_axis=1,
        tiled=True,
    )
    context_heads, log_total = attend(by_head[0], by_head[1], by_head[2])
    context = lax.all_to_all(context_heads, "seq", split_axis=0, concat_axis=1, tiled=True)
    middle = residual + matmul(context, params[7]) + params[8].astype(jnp.float32)
    mid_wide, normed_mid, inv_mid = layer_norm(middle, params[9], params[10])
    hidden_mid = mid_wide.astype(jnp.bfloat16)
    pre_act = matmul(hidden_mid, params[11]) + params[12].astype(jnp.float32)
    activated = gelu_exact(pre_act).astype(jnp.bfloat16)
    result = middle + matmul(activated, params[13]) + params[14].astype(jnp.float32)
    return (
        result,
        (
            hidden,
            normed_in,
            inv_in,
            by_head,
            log_total,
            context,
            normed_mid,
            inv_mid,
            hidden_mid,
            pre_act,
            activated,
        ),
    )


def backward_layer(upstream, stored, params):
    (
        hidden,
        normed_in,
        inv_in,
        by_head,
        log_total,
        context,
        normed_mid,
        inv_mid,
        hidden_mid,
        pre_act,
        activated,
    ) = stored
    upstream_low = upstream.astype(jnp.bfloat16)
    down_weight_gradient = contract_rows(activated, upstream_low)
    down_bias_gradient = jnp.sum(upstream, axis=0)
    pre_gradient = contract_cols(upstream_low, params[13]) * gelu_slope(pre_act)
    pre_low = pre_gradient.astype(jnp.bfloat16)
    up_weight_gradient = contract_rows(hidden_mid, pre_low)
    up_bias_gradient = jnp.sum(pre_gradient, axis=0)
    mid_hidden_gradient = contract_cols(pre_low, params[11])
    second_gain_gradient = jnp.sum(mid_hidden_gradient * normed_mid, axis=0)
    second_bias_gradient = jnp.sum(mid_hidden_gradient, axis=0)
    middle_gradient = upstream + norm_grad(mid_hidden_gradient, normed_mid, inv_mid, params[9])
    middle_low = middle_gradient.astype(jnp.bfloat16)
    out_weight_gradient = contract_rows(context, middle_low)
    out_bias_gradient = jnp.sum(middle_gradient, axis=0)
    context_gradient = contract_cols(middle_low, params[7]).astype(jnp.bfloat16)
    head_gradient = lax.all_to_all(context_gradient, "seq", split_axis=1, concat_axis=0, tiled=True)
    head_parts = attend_back(by_head[0], by_head[1], by_head[2], log_total, head_gradient)
    frame_parts = lax.all_to_all(head_parts, "seq", split_axis=1, concat_axis=2, tiled=True)
    query_gradient = frame_parts[0]
    key_gradient = frame_parts[1]
    value_gradient = frame_parts[2]
    query_weight_gradient = contract_rows(hidden, query_gradient)
    query_bias_gradient = jnp.sum(query_gradient.astype(jnp.float32), axis=0)
    key_weight_gradient = contract_rows(hidden, key_gradient)
    value_weight_gradient = contract_rows(hidden, value_gradient)
    value_bias_gradient = jnp.sum(value_gradient.astype(jnp.float32), axis=0)
    hidden_gradient = (
        contract_cols(query_gradient, params[2])
        + contract_cols(key_gradient, params[4])
        + contract_cols(value_gradient, params[5])
    )
    first_gain_gradient = jnp.sum(hidden_gradient * normed_in, axis=0)
    first_bias_gradient = jnp.sum(hidden_gradient, axis=0)
    input_gradient = middle_gradient + norm_grad(hidden_gradient, normed_in, inv_in, params[0])
    return (
        input_gradient,
        (
            first_gain_gradient,
            first_bias_gradient,
            query_weight_gradient,
            query_bias_gradient,
            key_weight_gradient,
            value_weight_gradient,
            value_bias_gradient,
            out_weight_gradient,
            out_bias_gradient,
            second_gain_gradient,
            second_bias_gradient,
            up_weight_gradient,
            up_bias_gradient,
            down_weight_gradient,
            down_bias_gradient,
        ),
    )


def reduce_gradients(gradients):
    shards = (
        lax.psum_scatter(gradients[0], "fsdp", scatter_dimension=0, tiled=True),
        lax.psum_scatter(gradients[1], "fsdp", scatter_dimension=0, tiled=True),
        lax.psum_scatter(gradients[2], "fsdp", scatter_dimension=0, tiled=True),
        lax.psum_scatter(gradients[3], "fsdp", scatter_dimension=0, tiled=True),
        lax.psum_scatter(gradients[4], "fsdp", scatter_dimension=0, tiled=True),
        lax.psum_scatter(gradients[5], "fsdp", scatter_dimension=0, tiled=True),
        lax.psum_scatter(gradients[6], "fsdp", scatter_dimension=0, tiled=True),
        lax.psum_scatter(gradients[7], "fsdp", scatter_dimension=0, tiled=True),
        lax.psum_scatter(gradients[8], "fsdp", scatter_dimension=0, tiled=True),
        lax.psum_scatter(gradients[9], "fsdp", scatter_dimension=0, tiled=True),
        lax.psum_scatter(gradients[10], "fsdp", scatter_dimension=0, tiled=True),
        lax.psum_scatter(gradients[11], "fsdp", scatter_dimension=0, tiled=True),
        lax.psum_scatter(gradients[12], "fsdp", scatter_dimension=0, tiled=True),
        lax.psum_scatter(gradients[13], "fsdp", scatter_dimension=0, tiled=True),
        lax.psum_scatter(gradients[14], "fsdp", scatter_dimension=0, tiled=True),
    )
    parts = (
        lax.psum_scatter(shards[0], "seq", scatter_dimension=0, tiled=True),
        lax.psum_scatter(shards[1], "seq", scatter_dimension=0, tiled=True),
        lax.psum_scatter(shards[2], "seq", scatter_dimension=0, tiled=True),
        lax.psum_scatter(shards[3], "seq", scatter_dimension=0, tiled=True),
        lax.psum_scatter(shards[4], "seq", scatter_dimension=0, tiled=True),
        lax.psum_scatter(shards[5], "seq", scatter_dimension=0, tiled=True),
        lax.psum_scatter(shards[6], "seq", scatter_dimension=0, tiled=True),
        lax.psum_scatter(shards[7], "seq", scatter_dimension=0, tiled=True),
        lax.psum_scatter(shards[8], "seq", scatter_dimension=0, tiled=True),
        lax.psum_scatter(shards[9], "seq", scatter_dimension=0, tiled=True),
        lax.psum_scatter(shards[10], "seq", scatter_dimension=0, tiled=True),
        lax.psum_scatter(shards[11], "seq", scatter_dimension=0, tiled=True),
        lax.psum_scatter(shards[12], "seq", scatter_dimension=0, tiled=True),
        lax.psum_scatter(shards[13], "seq", scatter_dimension=0, tiled=True),
        lax.psum_scatter(shards[14], "seq", scatter_dimension=0, tiled=True),
    )
    return (
        lax.all_gather(parts[0], "seq", axis=0, tiled=True),
        lax.all_gather(parts[1], "seq", axis=0, tiled=True),
        lax.all_gather(parts[2], "seq", axis=0, tiled=True),
        lax.all_gather(parts[3], "seq", axis=0, tiled=True),
        lax.all_gather(parts[4], "seq", axis=0, tiled=True),
        lax.all_gather(parts[5], "seq", axis=0, tiled=True),
        lax.all_gather(parts[6], "seq", axis=0, tiled=True),
        lax.all_gather(parts[7], "seq", axis=0, tiled=True),
        lax.all_gather(parts[8], "seq", axis=0, tiled=True),
        lax.all_gather(parts[9], "seq", axis=0, tiled=True),
        lax.all_gather(parts[10], "seq", axis=0, tiled=True),
        lax.all_gather(parts[11], "seq", axis=0, tiled=True),
        lax.all_gather(parts[12], "seq", axis=0, tiled=True),
        lax.all_gather(parts[13], "seq", axis=0, tiled=True),
        lax.all_gather(parts[14], "seq", axis=0, tiled=True),
    )


def on_device(
    frames_in,
    cotangent,
    first_gain,
    first_bias,
    query_weight,
    query_bias,
    key_weight,
    value_weight,
    value_bias,
    out_weight,
    out_bias,
    second_gain,
    second_bias,
    up_weight,
    up_bias,
    down_weight,
    down_bias,
):
    stacks = (
        first_gain,
        first_bias,
        query_weight,
        query_bias,
        key_weight,
        value_weight,
        value_bias,
        out_weight,
        out_bias,
        second_gain,
        second_bias,
        up_weight,
        up_bias,
        down_weight,
        down_bias,
    )
    layer_count = first_gain.shape[0]
    residual = frames_in[0]
    layer_num = 0
    params = gather_layer([stack[layer_num] for stack in stacks])
    residual, stored = forward_layer(residual, params)
    stored_all = [stored]
    gathered = [params]
    upstream = cotangent[0]
    reduced = [None] * layer_count
    for layer_num in reversed(range(layer_count)):
        params = gathered[layer_num]
        upstream, gradients = backward_layer(upstream, stored_all[layer_num], params)
        reduced[layer_num] = reduce_gradients(gradients)
    results = [residual[None], upstream[None]]
    for member in range(len(stacks)):
        results.append(jnp.stack([reduced[0][member]]))
    return tuple(results)


def solution(mesh):
    return jax.shard_map(
        on_device,
        mesh=mesh,
        in_specs=(
            P("fsdp", "seq", None),
            P("fsdp", "seq", None),
            P(None, "fsdp"),
            P(None, "fsdp"),
            P(None, "fsdp", None),
            P(None, "fsdp"),
            P(None, "fsdp", None),
            P(None, "fsdp", None),
            P(None, "fsdp"),
            P(None, "fsdp", None),
            P(None, "fsdp"),
            P(None, "fsdp"),
            P(None, "fsdp"),
            P(None, "fsdp", None),
            P(None, "fsdp"),
            P(None, "fsdp", None),
            P(None, "fsdp"),
        ),
        out_specs=(
            P("fsdp", "seq", None),
            P("fsdp", "seq", None),
            P(None, "fsdp"),
            P(None, "fsdp"),
            P(None, "fsdp", None),
            P(None, "fsdp"),
            P(None, "fsdp", None),
            P(None, "fsdp", None),
            P(None, "fsdp"),
            P(None, "fsdp", None),
            P(None, "fsdp"),
            P(None, "fsdp"),
            P(None, "fsdp"),
            P(None, "fsdp", None),
            P(None, "fsdp"),
            P(None, "fsdp", None),
            P(None, "fsdp"),
        ),
        check_vma=False,
    )
```

profile of v0, /device:TPU:0, one launch (start us, length us, event | category | flops | bytes accessed | tf_op | source)
XLA Modules:
  0.0 885.4 jit_solution(2830720401970173773)
XLA Ops:
  21.5 63.2 %all-reduce.39 = (bf16[768]{0:T(1024)(128)(2,1)S(1)}, bf16[768]{0:T(1024)(128)(2,1)S(1)}, bf16[768]{0:T(1024)(128)(2,1)S(1)}, bf16[768]{0:T(1024)(128)(2,1)S(1)}...) all-reduce(bf16[768]{0:T(1024)(128)(2,1)S(1)} %dynamic-update-slice, ...), channel_id=3, replica_groups=mesh['seq'=2,'fsdp'=16] {'fsdp'}, use_global_device_ids=true, to_apply=%add.1 | all-reduce | flops 9216 | bytes 36864
  87.7 3.1 all-gather.26.cloned.1.call-done
  92.5 37.9 %all-gather.22.cloned.1.call-done = bf16[1,768,768]{2,1,0:T(8,128)(2,1)} async-done(((bf16[1,48,768]{2,1,0:T(8,128)(2,1)}), bf16[1,768,768]{2,1,0:T(8,128)(2,1)}) %all-gather.22.cloned.1.call-update) | async-done | bytes 1179664 | tf_op jit(solution)/shard_map/all_gather | solution.py:117
  132.7 13.9 %all_to_all.62 = bf16[3,128,768]{1,0,2:T(4,128)(2,1)S(1)} all-to-all(bf16[3,128,768]{1,0,2:T(4,128)(2,1)S(1)} %copy.66), channel_id=1, replica_groups=mesh['seq'=2,'fsdp'=16] {'seq'}, dimensions={2} | all-to-all | bytes 1179648 | tf_op jit(solution)/shard_map/all_to_all | solution.py:139
  150.6 3.4 all-to-all-start.1
  154.1 15.5 %all-gather.28.cloned.1.call-done = bf16[1,768,768]{2,1,0:T(8,128)(2,1)} async-done(((bf16[1,48,768]{2,1,0:T(8,128)(2,1)}), bf16[1,768,768]{2,1,0:T(8,128)(2,1)}) %all-gather.28.cloned.1.call-update) | async-done | bytes 1179664 | tf_op jit(solution)/shard_map/all_gather | solution.py:122
  171.6 52.2 %all-gather.30.cloned.1.call-done = bf16[1,768,3072]{2,1,0:T(8,128)(2,1)} async-done(((bf16[1,48,3072]{2,1,0:T(8,128)(2,1)}), bf16[1,768,3072]{2,1,0:T(8,128)(2,1)}) %all-gather.30.cloned.1.call-update) | async-done | bytes 4718608 | tf_op jit(solution)/shard_map/all_gather | solution.py:126
  223.8 4.4 fusion.9
  228.1 49.5 %all-gather.32.cloned.1.call-done = bf16[1,3072,768]{2,1,0:T(8,128)(2,1)} async-done(((bf16[1,192,768]{2,1,0:T(8,128)(2,1)}), bf16[1,3072,768]{2,1,0:T(8,128)(2,1)}) %all-gather.32.cloned.1.call-update) | async-done | bytes 4718608 | tf_op jit(solution)/shard_map/all_gather | solution.py:128
  277.6 5.3 fusion.108
  282.9 2.3 multiply_reduce_fusion.1
  286.7 1.9 fusion.92
  288.7 1.8 fusion.58
  290.6 7.5 all_to_all.63
  300.0 1.8 convolution_convert_fusion
  301.8 1.9 copy.77
  305.2 2.7 fusion.52
  309.0 3.4 fusion.49
  313.7 2.4 pad_maximum_fusion
  316.1 12.9 %all_to_all.64 = bf16[3,256,384]{2,0,1:T(4,128)(2,1)S(1)} all-to-all(bf16[3,256,384]{2,0,1:T(4,128)(2,1)S(1)} %pad_maximum_fusion), channel_id=1, replica_groups=mesh['seq'=2,'fsdp'=16] {'seq'}, dimensions={1} | all-to-all | bytes 1179648 | tf_op jit(solution)/shard_map/all_to_all | solution.py:203
  330.1 2.0 fusion.115
  332.4 2.1 fusion.113
  334.8 2.0 fusion.111
  338.0 5.2 fusion.84
  344.6 5.1 fusion.91
  350.6 65.9 %reduce-scatter.13.cloned.1.call-done = f32[48,768]{1,0:T(8,128)} async-done(((f32[768,768]{1,0:T(8,128)}), f32[48,768]{1,0:T(8,128)}) %reduce-scatter.13.cloned.1.call-update) | async-done | bytes 147472 | tf_op jit(solution)/shard_map/reduce_scatter | solution.py:246
  420.6 62.0 %reduce-scatter.17.cloned.1.call-done = f32[48,768]{1,0:T(8,128)} async-done(((f32[768,768]{1,0:T(8,128)}), f32[48,768]{1,0:T(8,128)}) %reduce-scatter.17.cloned.1.call-update) | async-done | bytes 147472 | tf_op jit(solution)/shard_map/reduce_scatter | solution.py:248
  482.7 4.0 fusion.35
  486.6 61.8 %reduce-scatter.21.cloned.1.call-done = f32[48,768]{1,0:T(8,128)} async-done(((f32[768,768]{1,0:T(8,128)}), f32[48,768]{1,0:T(8,128)}) %reduce-scatter.21.cloned.1.call-update) | async-done | bytes 147472 | tf_op jit(solution)/shard_map/reduce_scatter | solution.py:249
  548.5 1.8 fusion.46
  550.4 2.3 convolution_add_fusion.1
  552.7 110.2 %reduce-scatter.29.cloned.1.call-done = f32[48,3072]{1,0:T(8,128)} async-done(((f32[768,3072]{1,0:T(8,128)}), f32[48,3072]{1,0:T(8,128)}) %reduce-scatter.29.cloned.1.call-update) | async-done | bytes 589840 | tf_op jit(solution)/shard_map/reduce_scatter | solution.py:255
  665.8 62.5 %all-reduce.36 = (f32[768]{0:T(1024)S(1)}, f32[768]{0:T(1024)S(1)}, f32[768]{0:T(1024)S(1)}, f32[768]{0:T(1024)S(1)}, f32[768]{0:T(1024)S(1)}, /*index=5*/f32[76...) all-reduce(f32[768]{0:T(1024)S(1)} %get-tuple-element.19, ...), channel_id=17, replica_groups=mesh['seq'=2,'fsdp'=16] {'fsdp'}, use_global_device_ids=true, to_apply=%region_12.0.clone | all-reduce | flops 9216 | bytes 73728
  729.0 5.0 all-reduce.38
  735.1 44.5 %reduce-scatter.33.cloned.1.call-done = f32[192,768]{1,0:T(8,128)} async-done(((f32[3072,768]{1,0:T(8,128)}), f32[192,768]{1,0:T(8,128)}) %reduce-scatter.33.cloned.1.call-update) | async-done | bytes 589840 | tf_op jit(solution)/shard_map/reduce_scatter | solution.py:257
  779.9 5.5 all-reduce.37
  786.4 5.6 reduce-scatter.27.cloned.1.call-done
  792.0 5.2 all_gather.112
  797.2 7.4 reduce-scatter.15.cloned.1.call-done
  804.6 5.2 all_gather.107
  809.8 7.4 reduce-scatter.19.cloned.1.call-done
  817.2 5.2 all_gather.109
  822.5 7.4 reduce-scatter.23.cloned.1.call-done
  829.9 5.2 all_gather.110
  835.1 12.3 %reduce-scatter.31.cloned.1.call-done = f32[24,3072]{1,0:T(8,128)} async-done(((f32[48,3072]{1,0:T(8,128)}), f32[24,3072]{1,0:T(8,128)}) %reduce-scatter.31.cloned.1.call-update) | async-done | bytes 294928 | tf_op jit(solution)/shard_map/reduce_scatter | solution.py:272
  847.3 9.5 %all_gather.116 = f32[48,3072]{1,0:T(8,128)S(1)} all-gather(f32[24,3072]{1,0:T(8,128)} %reduce-scatter.31.cloned.1.call-done), channel_id=1, replica_groups=mesh['seq'=2,'fsdp'=16] {'seq'}, dimensions={0}, use_global_device_ids=true | all-gather | bytes 884736 | tf_op jit(solution)/shard_map/all_gather | solution.py:289
  856.8 8.0 reduce-scatter.35.cloned.1.call-done
  864.9 9.5 %all_gather.118 = f32[192,768]{1,0:T(8,128)S(1)} all-gather(f32[96,768]{1,0:T(8,128)} %reduce-scatter.35.cloned.1.call-done), channel_id=1, replica_groups=mesh['seq'=2,'fsdp'=16] {'seq'}, dimensions={0}, use_global_device_ids=true | all-gather | bytes 884736 | tf_op jit(solution)/shard_map/all_gather | solution.py:291
  (205 shorter events, 48.6 us)
Async XLA Ops:
  7.2 78.6 %copy-start = (f32[1,128,768]{2,1,0:T(8,128)S(1)}, f32[1,128,768]{2,1,0:T(8,128)}, u32[]{:S(2)}) copy-start(f32[1,128,768]{2,1,0:T(8,128)} %param.17) | copy-start | bytes 1179652
  7.2 78.9 %all-gather.24.cloned.1.call-start = ((), (), s32[]{:S(2)}) async-start(), calls=%async_computation.29 | async-start | bytes 1253376 | tf_op jit(solution)/shard_map/all_gather | solution.py:119
  7.9 82.9 %all-gather.26.cloned.1.call-start = ((), (), s32[]{:S(2)}) async-start(), calls=%async_computation.30 | async-start | bytes 1253376 | tf_op jit(solution)/shard_map/all_gather | solution.py:120
  8.7 121.7 %all-gather.22.cloned.1.call-start = ((), (), s32[]{:S(2)}) async-start(), calls=%async_computation.28 | async-start | bytes 1253376 | tf_op jit(solution)/shard_map/all_gather | solution.py:117
  9.4 160.2 %all-gather.28.cloned.1.call-start = ((), (), s32[]{:S(2)}) async-start(), calls=%async_computation.31 | async-start | bytes 1253376 | tf_op jit(solution)/shard_map/all_gather | solution.py:122
  10.0 213.8 %all-gather.30.cloned.1.call-start = ((), (), s32[]{:S(2)}) async-start(), calls=%async_computation.32 | async-start | bytes 5013504 | tf_op jit(solution)/shard_map/all_gather | solution.py:126
  10.6 267.0 %all-gather.32.cloned.1.call-start = ((), (), s32[]{:S(2)}) async-start(), calls=%async_computation.33 | async-start | bytes 5013504 | tf_op jit(solution)/shard_map/all_gather | solution.py:128
  85.8 44.5 %copy-start.14 = (f32[128]{0:T(128)}, f32[128]{0:T(128)S(1)}, u32[]{:S(2)}) copy-start(f32[128]{0:T(128)S(1)} %broadcast_multiply_fusion.5) | copy-start | bytes 1540
  86.0 44.3 %copy-start.17 = (f32[128]{0:T(128)}, f32[128]{0:T(128)S(1)}, u32[]{:S(2)}) copy-start(f32[128]{0:T(128)S(1)} %add_rsqrt_fusion.1) | copy-start | bytes 1540
  148.0 0.8 copy-start.12
  148.1 0.7 copy-start.11
  148.8 0.6 copy-start.13
  150.6 19.0 %all-to-all-start.1 = ((bf16[2,128,384]{1,2,0:T(8,128)(2,1)}), bf16[2,128,384]{1,2,0:T(8,128)(2,1)S(1)}, u32[]{:S(2)}, u32[]{:S(2)}) async-start(bf16[2,128,384]{1,2,0:T(8,128)(2,1)} %copy.69), calls=%async_computation.1 | async-start | bytes 393216 | tf_op jit(solution)/shard_map/all_to_all | solution.py:147
  154.0 196.5 %reduce-scatter.25.cloned.1.call-start = ((), (), s32[]{:S(2)}) async-start(), calls=%async_computation.22 | async-start | bytes 2506752 | tf_op jit(solution)/shard_map/reduce_scatter | solution.py:251
  171.3 111.6 %copy-start.20 = (f32[128]{0:T(128)}, f32[128]{0:T(128)S(1)}, u32[]{:S(2)}) copy-start(f32[128]{0:T(128)S(1)} %broadcast_multiply_fusion.4) | copy-start | bytes 1540
  171.5 111.4 %copy-start.25 = (f32[128]{0:T(128)}, f32[128]{0:T(128)S(1)}, u32[]{:S(2)}) copy-start(f32[128]{0:T(128)S(1)} %add_rsqrt_fusion) | copy-start | bytes 1540
  171.5 106.1 %copy-start.6 = (f32[1,128,768]{2,1,0:T(8,128)S(1)}, f32[1,128,768]{2,1,0:T(8,128)}, u32[]{:S(2)}) copy-start(f32[1,128,768]{2,1,0:T(8,128)} %param.18) | copy-start | bytes 1179652
  277.6 5.3 copy-start.2
  282.9 2.3 copy-start.7
  288.7 127.9 %reduce-scatter.13.cloned.1.call-start = ((), (), s32[]{:S(2)}) async-start(), calls=%async_computation.16 | async-start | bytes 2506752 | tf_op jit(solution)/shard_map/reduce_scatter | solution.py:246
  309.0 4.7 copy-start.10
  329.0 1.1 copy-start.15
  329.0 1.2 copy-start.18
  329.1 0.8 copy-start.5
  332.2 150.4 %reduce-scatter.17.cloned.1.call-start = ((), (), s32[]{:S(2)}) async-start(), calls=%async_computation.18 | async-start | bytes 2506752 | tf_op jit(solution)/shard_map/reduce_scatter | solution.py:248
  332.4 2.2 copy-start.9
  334.6 213.9 %reduce-scatter.21.cloned.1.call-start = ((), (), s32[]{:S(2)}) async-start(), calls=%async_computation.20 | async-start | bytes 2506752 | tf_op jit(solution)/shard_map/reduce_scatter | solution.py:249
  336.8 1.1 copy-start.8
  336.8 1.1 copy-start.21
  336.8 1.1 copy-start.26
  336.9 326.0 %reduce-scatter.29.cloned.1.call-start = ((), (), s32[]{:S(2)}) async-start(), calls=%async_computation.24 | async-start | bytes 10027008 | tf_op jit(solution)/shard_map/reduce_scatter | solution.py:255
  343.1 1.4 copy-start.1
  343.2 436.4 %reduce-scatter.33.cloned.1.call-start = ((), (), s32[]{:S(2)}) async-start(), calls=%async_computation.26 | async-start | bytes 10027008 | tf_op jit(solution)/shard_map/reduce_scatter | solution.py:257
  349.6 67.0 %copy-start.28 = (bf16[768]{0:T(1024)(128)(2,1)S(1)}, bf16[768]{0:T(1024)(128)(2,1)}, u32[]{:S(2)}) copy-start(bf16[768]{0:T(1024)(128)(2,1)} %get-tuple-element.59) | copy-start | bytes 4612
  349.6 442.4 %reduce-scatter.27.cloned.1.call-start = ((), (), s32[]{:S(2)}) async-start(), calls=%async_computation.23 | async-start | bytes 221184 | tf_op jit(solution)/shard_map/reduce_scatter | solution.py:268
  350.6 454.0 %reduce-scatter.15.cloned.1.call-start = ((), (), s32[]{:S(2)}) async-start(), calls=%async_computation.17 | async-start | bytes 221184 | tf_op jit(solution)/shard_map/reduce_scatter | solution.py:263
  416.6 400.6 %reduce-scatter.19.cloned.1.call-start = ((), (), s32[]{:S(2)}) async-start(), calls=%async_computation.19 | async-start | bytes 221184 | tf_op jit(solution)/shard_map/reduce_scatter | solution.py:265
  482.6 347.2 %reduce-scatter.23.cloned.1.call-start = ((), (), s32[]{:S(2)}) async-start(), calls=%async_computation.21 | async-start | bytes 221184 | tf_op jit(solution)/shard_map/reduce_scatter | solution.py:266
  486.6 63.7 %copy-start.4 = (bf16[1,768,768]{2,1,0:T(8,128)(2,1)S(1)}, bf16[1,768,768]{2,1,0:T(8,128)(2,1)}, u32[]{:S(2)}) copy-start(bf16[1,768,768]{2,1,0:T(8,128)(2,1)} %all-gather.24.cloned.1.call-done) | copy-start | bytes 3538948
  548.5 298.9 %reduce-scatter.31.cloned.1.call-start = ((), (), s32[]{:S(2)}) async-start(), calls=%async_computation.25 | async-start | bytes 884736 | tf_op jit(solution)/shard_map/reduce_scatter | solution.py:272
  550.4 113.7 %copy-start.3 = (bf16[1,768,768]{2,1,0:T(8,128)(2,1)S(1)}, bf16[1,768,768]{2,1,0:T(8,128)(2,1)}, u32[]{:S(2)}) copy-start(bf16[1,768,768]{2,1,0:T(8,128)(2,1)} %all-gather.26.cloned.1.call-done) | copy-start | bytes 3538948
  550.4 113.7 %copy-start.16 = (f32[128]{0:T(128)S(1)}, f32[128]{0:T(128)}, u32[]{:S(2)}) copy-start(f32[128]{0:T(128)} %copy-done.14) | copy-start | bytes 1540
  550.4 113.7 %copy-start.19 = (f32[128]{0:T(128)S(1)}, f32[128]{0:T(128)}, u32[]{:S(2)}) copy-start(f32[128]{0:T(128)} %copy-done.17) | copy-start | bytes 1540
  662.9 2.9 copy-start.22
  662.9 2.9 copy-start.23
  662.9 2.9 copy-start.24
  662.9 2.9 copy-start.27
  662.9 201.9 %reduce-scatter.35.cloned.1.call-start = ((), (), s32[]{:S(2)}) async-start(), calls=%async_computation.27 | async-start | bytes 884736 | tf_op jit(solution)/shard_map/reduce_scatter | solution.py:274
Sparse Core Ops, SparseCore 0:
  10.3 41.0 all-gather.23
  53.7 37.1 all-gather.25
  93.1 37.1 all-gather.21
  132.5 37.0 all-gather.27
  171.7 51.9 all-gather.29
  225.9 51.6 all-gather.31
  288.8 61.7 reduce-scatter.24
  354.3 62.1 reduce-scatter.12
  420.3 62.1 reduce-scatter.16
  486.2 62.2 reduce-scatter.20
  552.6 110.2 reduce-scatter.28
  666.8 112.7 reduce-scatter.32
  781.8 10.1 reduce-scatter.26
  794.1 10.5 reduce-scatter.14
  806.7 10.5 reduce-scatter.18
  819.3 10.5 reduce-scatter.22
  832.0 15.3 reduce-scatter.30
  849.5 15.3 reduce-scatter.34
where the time goes:
time: 887 us; the launch traced here: 885 us
  waiting for transfers between devices  555 us (63%)
  blocking collectives  210 us (24%)
  matrix products  58.7 us (7%)
  local copies, waits for them, and re-layouts  28.3 us (3%)
  between operations  20.1 us (2%)
    unnamed x4, blocking collectives  136 us
    reduce_scatter x1, waiting for transfers between devices, reduce_gradients(): lax.psum_scatter(gradients[11], 'fsdp', scatter_dimension=0, tiled=True)  110 us
    reduce_scatter x1, waiting for transfers between devices, reduce_gradients(): lax.psum_scatter(gradients[2], 'fsdp', scatter_dimension=0, tiled=True)  65.9 us
    reduce_scatter x1, waiting for transfers between devices, reduce_gradients(): lax.psum_scatter(gradients[4], 'fsdp', scatter_dimension=0, tiled=True)  62 us
    reduce_scatter x1, waiting for transfers between devices, reduce_gradients(): lax.psum_scatter(gradients[5], 'fsdp', scatter_dimension=0, tiled=True)  61.8 us
    all_gather x1, waiting for transfers between devices, gather_layer(): lax.all_gather(shards[11], 'fsdp', axis=0, tiled=True)  52.2 us
    all_gather x1, waiting for transfers between devices, gather_layer(): lax.all_gather(shards[13], 'fsdp', axis=0, tiled=True)  49.5 us
    reduce_scatter x1, waiting for transfers between devices, reduce_gradients(): lax.psum_scatter(gradients[13], 'fsdp', scatter_dimension=0, tiled=True)  44.5 us
  transfers between devices with their start and end apart: 19, of which 17 were waited for; matrix products, arithmetic and copies ran while one was open for 9% of the time, Pallas kernels for 0%

commit v1 on v0

--- a/solution.py
+++ b/solution.py
@@ -1,3 +1,4 @@
+import functools
 import jax
 import jax.numpy as jnp
 from jax import lax
@@ -7,6 +8,33 @@
 EPSILON = 1e-05
 ROOT_HALF = 0.7071067811865476
 INV_ROOT_TAU = 0.3989422804014327
+
+
+def _wait_view(my_tile, where_dim):
+    low = list(my_tile.shape[1:])
+    low[where_dim] *= my_tile.shape[0]
+    return jnp.moveaxis(my_tile, 0, where_dim).reshape(low)
+
+
+def define_knots_for(array_here, which_axis, array_axis):
+    degree = jax.lax.axis_size(which_axis)
+    made = [(idx, (idx + 1) % degree) for idx in range(degree)]
+    items = [(it, c) for c, it in made]
+    vec_out, placed = ([], [])
+    for d in range(degree - 1):
+        if d % 2 == 0:
+            vec_out.append(
+                jax.lax.ppermute(vec_out[-1] if vec_out else array_here, which_axis, made)
+            )
+        else:
+            placed.append(jax.lax.ppermute(placed[-1] if placed else array_here, which_axis, items))
+    state_next = jnp.stack([*vec_out[::-1], array_here, *placed])
+    local_out = jax.lax.axis_index(which_axis) - len(vec_out)
+    state_next = state_next[(jnp.arange(degree) - local_out) % degree]
+    return _wait_view(state_next, array_axis)
+
+
+form_values_over_axis = functools.partial(define_knots_for, which_axis="fsdp", array_axis=0)
 
 
 def matmul(left, right):
@@ -125,7 +153,7 @@
         lax.all_gather(shards[10], "fsdp", axis=0, tiled=True),
         lax.all_gather(shards[11], "fsdp", axis=0, tiled=True),
         lax.all_gather(shards[12], "fsdp", axis=0, tiled=True),
-        lax.all_gather(shards[13], "fsdp", axis=0, tiled=True),
+        form_values_over_axis(shards[13]),
         lax.all_gather(shards[14], "fsdp", axis=0, tiled=True),
     )
 

time: 887 us -> 845 us (0.953)
  waiting for transfers between devices: 555 us -> 470 us
  starting transfers between devices: 4.15 us -> 37.9 us
  local copies, waits for them, and re-layouts: 28.3 us -> 50.6 us
  blocking collectives: 210 us -> 195 us
    all_gather x1 -> x0, waiting for transfers between devices: 49.5 us -> none  [gather_layer(): lax.all_gather(shards[13], 'fsdp', axis=0, tiled=True)]
    all_gather x1, waiting for transfers between devices: 37.9 us -> 0.02 us  [gather_layer(): lax.all_gather(shards[2], 'fsdp', axis=0, tiled=True)]
    ppermute x0 -> x15, starting transfers between devices: none -> 29.9 us  [the longest x7 27.9 us: define_knots_for(): jax.lax.ppermute(placed[-1] if placed else array_here, which_axis, items)]
    ppermute x0 -> x15, waiting for transfers between devices: none -> 25.8 us  [the longest x8 21.5 us: define_knots_for(): jax.lax.ppermute(vec_out[-1] if vec_out else array_here, which_axis, made)]
    all_gather x1, waiting for transfers between devices: 15.5 us -> 0.01 us  [gather_layer(): lax.all_gather(shards[7], 'fsdp', axis=0, tiled=True)]
    unnamed x110 -> x147, local copies, waits for them, and re-layouts: 18.6 us -> 32.9 us
    all_to_all x1 -> x0, blocking collectives: 13.9 us -> none  [forward_layer(): lax.all_to_all(jnp.stack([query_rows, key_rows, value_rows]), 'seq', spli...]
  transfers between devices with their start and end apart: 19 -> 34, of which waited for: 17 -> 22; matrix products, arithmetic and copies ran while one was open for 9% -> 12% of each run, Pallas kernels for 0% -> 0%
where the time goes in v1:
time: 845 us; the launch traced here: 843 us
  waiting for transfers between devices  470 us (56%)
  blocking collectives  195 us (23%)
  matrix products  57.7 us (7%)
  local copies, waits for them, and re-layouts  50.6 us (6%)
  starting transfers between devices  37.9 us (4%)
  between operations  19.9 us (2%)
  other arithmetic  11.3 us (1%)
    unnamed x4, blocking collectives  135 us
    reduce_scatter x1, waiting for transfers between devices, reduce_gradients(): lax.psum_scatter(gradients[11], 'fsdp', scatter_dimension=0, tiled=True)  110 us
    reduce_scatter x1, waiting for transfers between devices, reduce_gradients(): lax.psum_scatter(gradients[2], 'fsdp', scatter_dimension=0, tiled=True)  66 us
    reduce_scatter x1, waiting for transfers between devices, reduce_gradients(): lax.psum_scatter(gradients[4], 'fsdp', scatter_dimension=0, tiled=True)  62 us
    reduce_scatter x1, waiting for transfers between devices, reduce_gradients(): lax.psum_scatter(gradients[5], 'fsdp', scatter_dimension=0, tiled=True)  62 us
    all_gather x1, waiting for transfers between devices, gather_layer(): lax.all_gather(shards[11], 'fsdp', axis=0, tiled=True)  47.4 us
    reduce_scatter x1, waiting for transfers between devices, reduce_gradients(): lax.psum_scatter(gradients[13], 'fsdp', scatter_dimension=0, tiled=True)  44.8 us
    unnamed x147, local copies, waits for them, and re-layouts  32.9 us
  transfers between devices with their start and end apart: 34, of which 22 were waited for; matrix products, arithmetic and copies ran while one was open for 12% of the time, Pallas kernels for 0%

profile of v1, /device:TPU:0, one launch (start us, length us, event | category | flops | bytes accessed | tf_op | source)
XLA Modules:
  0.0 843.0 jit_solution(5659097234370245787)
XLA Ops:
  11.1 5.0 collective-permute-start.8
  16.2 4.7 collective-permute-done
  20.9 4.4 collective-permute-start.9
  25.3 5.9 collective-permute-done.1
  31.2 4.4 collective-permute-start.10
  35.7 4.5 collective-permute-done.2
  41.7 4.6 collective-permute-start.11
  46.3 3.4 collective-permute-done.3
  51.2 4.6 collective-permute-start.12
  55.8 2.8 collective-permute-done.4
  69.0 62.3 %all-reduce.39 = (bf16[768]{0:T(1024)(128)(2,1)S(1)}, bf16[768]{0:T(1024)(128)(2,1)S(1)}, bf16[768]{0:T(1024)(128)(2,1)S(1)}, bf16[768]{0:T(1024)(128)(2,1)S(1)}...) all-reduce(bf16[768]{0:T(1024)(128)(2,1)S(1)} %dynamic-update-slice, ...), channel_id=3, replica_groups=mesh['seq'=2,'fsdp'=16] {'fsdp'}, use_global_device_ids=true, to_apply=%add.1 | all-reduce | flops 9216 | bytes 36864
  134.9 3.2 collective-permute-done.13
  138.1 4.8 collective-permute-start.14
  149.6 3.5 all-to-all-start
  171.7 3.4 all-to-all-start.1
  177.1 5.5 gather_fusion
  184.6 47.4 %all-gather.28.cloned.1.call-done = bf16[1,768,3072]{2,1,0:T(8,128)(2,1)} async-done(((bf16[1,48,3072]{2,1,0:T(8,128)(2,1)}), bf16[1,768,3072]{2,1,0:T(8,128)(2,1)}) %all-gather.28.cloned.1.call-update) | async-done | bytes 4718608 | tf_op jit(solution)/shard_map/all_gather | solution.py:154
  232.0 3.4 fusion.5
  235.4 5.3 fusion.98
  240.7 2.3 multiply_reduce_fusion.1
  248.3 7.5 all_to_all.62
  263.0 2.7 fusion.39
  266.8 3.4 fusion.36
  271.5 2.4 pad_maximum_fusion
  273.9 12.9 %all_to_all.63 = bf16[3,256,384]{2,0,1:T(4,128)(2,1)S(1)} all-to-all(bf16[3,256,384]{2,0,1:T(4,128)(2,1)S(1)} %pad_maximum_fusion), channel_id=1, replica_groups=mesh['seq'=2,'fsdp'=16] {'seq'}, dimensions={1} | all-to-all | bytes 1179648 | tf_op jit(solution)/shard_map/all_to_all | solution.py:231
  295.7 5.2 fusion.71
  302.3 5.1 fusion.78
  308.4 66.0 %reduce-scatter.13.cloned.1.call-done = f32[48,768]{1,0:T(8,128)} async-done(((f32[768,768]{1,0:T(8,128)}), f32[48,768]{1,0:T(8,128)}) %reduce-scatter.13.cloned.1.call-update) | async-done | bytes 147472 | tf_op jit(solution)/shard_map/reduce_scatter | solution.py:274
  378.3 62.0 %reduce-scatter.17.cloned.1.call-done = f32[48,768]{1,0:T(8,128)} async-done(((f32[768,768]{1,0:T(8,128)}), f32[48,768]{1,0:T(8,128)}) %reduce-scatter.17.cloned.1.call-update) | async-done | bytes 147472 | tf_op jit(solution)/shard_map/reduce_scatter | solution.py:276
  440.4 4.0 fusion.24
  444.4 62.0 %reduce-scatter.21.cloned.1.call-done = f32[48,768]{1,0:T(8,128)} async-done(((f32[768,768]{1,0:T(8,128)}), f32[48,768]{1,0:T(8,128)}) %reduce-scatter.21.cloned.1.call-update) | async-done | bytes 147472 | tf_op jit(solution)/shard_map/reduce_scatter | solution.py:277
  510.6 110.0 %reduce-scatter.29.cloned.1.call-done = f32[48,3072]{1,0:T(8,128)} async-done(((f32[768,3072]{1,0:T(8,128)}), f32[48,3072]{1,0:T(8,128)}) %reduce-scatter.29.cloned.1.call-update) | async-done | bytes 589840 | tf_op jit(solution)/shard_map/reduce_scatter | solution.py:283
  623.6 62.3 %all-reduce.36 = (f32[768]{0:T(1024)S(1)}, f32[768]{0:T(1024)S(1)}, f32[768]{0:T(1024)S(1)}, f32[768]{0:T(1024)S(1)}, f32[768]{0:T(1024)S(1)}, /*index=5*/f32[76...) all-reduce(f32[768]{0:T(1024)S(1)} %get-tuple-element.19, ...), channel_id=16, replica_groups=mesh['seq'=2,'fsdp'=16] {'fsdp'}, use_global_device_ids=true, to_apply=%region_12.13.clone | all-reduce | flops 9216 | bytes 73728
  686.6 5.0 all-reduce.38
  692.7 44.8 %reduce-scatter.33.cloned.1.call-done = f32[192,768]{1,0:T(8,128)} async-done(((f32[3072,768]{1,0:T(8,128)}), f32[192,768]{1,0:T(8,128)}) %reduce-scatter.33.cloned.1.call-update) | async-done | bytes 589840 | tf_op jit(solution)/shard_map/reduce_scatter | solution.py:285
  737.9 5.5 all-reduce.37
  744.3 5.4 reduce-scatter.27.cloned.1.call-done
  749.8 5.2 all_gather.108
  755.0 7.5 reduce-scatter.15.cloned.1.call-done
  762.5 5.2 all_gather.103
  767.8 7.4 reduce-scatter.19.cloned.1.call-done
  775.2 5.2 all_gather.105
  780.4 7.4 reduce-scatter.23.cloned.1.call-done
  787.8 5.2 all_gather.106
  793.0 12.3 %reduce-scatter.31.cloned.1.call-done = f32[24,3072]{1,0:T(8,128)} async-done(((f32[48,3072]{1,0:T(8,128)}), f32[24,3072]{1,0:T(8,128)}) %reduce-scatter.31.cloned.1.call-update) | async-done | bytes 294928 | tf_op jit(solution)/shard_map/reduce_scatter | solution.py:300
  805.3 9.5 %all_gather.112 = f32[48,3072]{1,0:T(8,128)S(1)} all-gather(f32[24,3072]{1,0:T(8,128)} %reduce-scatter.31.cloned.1.call-done), channel_id=1, replica_groups=mesh['seq'=2,'fsdp'=16] {'seq'}, dimensions={0}, use_global_device_ids=true | all-gather | bytes 884736 | tf_op jit(solution)/shard_map/all_gather | solution.py:317
  814.7 8.0 reduce-scatter.35.cloned.1.call-done
  822.8 9.5 %all_gather.114 = f32[192,768]{1,0:T(8,128)S(1)} all-gather(f32[96,768]{1,0:T(8,128)} %reduce-scatter.35.cloned.1.call-done), channel_id=1, replica_groups=mesh['seq'=2,'fsdp'=16] {'seq'}, dimensions={0}, use_global_device_ids=true | all-gather | bytes 884736 | tf_op jit(solution)/shard_map/all_gather | solution.py:319
  (275 shorter events, 89.0 us)
Async XLA Ops:
  7.2 135.9 %copy-start = (f32[1,128,768]{2,1,0:T(8,128)S(1)}, f32[1,128,768]{2,1,0:T(8,128)}, u32[]{:S(2)}) copy-start(f32[1,128,768]{2,1,0:T(8,128)} %param.17) | copy-start | bytes 1179652
  7.2 135.9 %all-gather.24.cloned.1.call-start = ((), (), s32[]{:S(2)}) async-start(), calls=%async_computation.30 | async-start | bytes 1253376 | tf_op jit(solution)/shard_map/all_gather | solution.py:148
  7.9 136.9 %all-gather.20.cloned.1.call-start = ((), (), s32[]{:S(2)}) async-start(), calls=%async_computation.28 | async-start | bytes 1253376 | tf_op jit(solution)/shard_map/all_gather | solution.py:145
  8.7 137.9 %all-gather.22.cloned.1.call-start = ((), (), s32[]{:S(2)}) async-start(), calls=%async_computation.29 | async-start | bytes 1253376 | tf_op jit(solution)/shard_map/all_gather | solution.py:147
  9.4 173.2 %all-gather.26.cloned.1.call-start = ((), (), s32[]{:S(2)}) async-start(), calls=%async_computation.31 | async-start | bytes 1253376 | tf_op jit(solution)/shard_map/all_gather | solution.py:150
  10.0 222.0 %all-gather.28.cloned.1.call-start = ((), (), s32[]{:S(2)}) async-start(), calls=%async_computation.32 | async-start | bytes 5013504 | tf_op jit(solution)/shard_map/all_gather | solution.py:154
  10.6 10.3 %collective-permute-start = (bf16[192,768]{1,0:T(8,128)(2,1)}, bf16[192,768]{1,0:T(8,128)(2,1)S(1)}, u32[]{:S(2)}, u32[]{:S(2)}) collective-permute-start(bf16[192,768]{1,0:T(8,128)(2,1)} %bitcast.251), channel_id=1, source_target_pairs={{0,1},{1,2},{2,3},{3,4},{4,5},{5,6},{6,7},{7,8},{8,9},{9,10},{10,1... | collective-permute-start | bytes 884744 | tf_op jit(solution)/shard_map/ppermute | solution.py:27
  11.1 9.8 %collective-permute-start.8 = (bf16[192,768]{1,0:T(8,128)(2,1)}, bf16[192,768]{1,0:T(8,128)(2,1)S(1)}, u32[]{:S(2)}, u32[]{:S(2)}) collective-permute-start(bf16[192,768]{1,0:T(8,128)(2,1)} %bitcast.252), channel_id=1, source_target_pairs={{1,0},{2,1},{3,2},{4,3},{5,4},{6,5},{7,6},{8,7},{9,8},{10,9},{11,1... | collective-permute-start | bytes 884744 | tf_op jit(solution)/shard_map/ppermute | solution.py:30
  20.8 10.4 %collective-permute-start.1 = (bf16[192,768]{1,0:T(8,128)(2,1)S(1)}, bf16[192,768]{1,0:T(8,128)(2,1)S(1)}, u32[]{:S(2)}, u32[]{:S(2)}) collective-permute-start(bf16[192,768]{1,0:T(8,128)(2,1)S(1)} %collective-permute-done), channel_id=1, source_target_pairs={{0,1},{1,2},{2,3},{3,4},{4,5},{5,6},{6,7},{7,8},{8,9},{9,10},{10,1... | collective-permute-start | bytes 884744 | tf_op jit(solution)/shard_map/ppermute | solution.py:27
  20.9 10.3 %collective-permute-start.9 = (bf16[192,768]{1,0:T(8,128)(2,1)S(1)}, bf16[192,768]{1,0:T(8,128)(2,1)S(1)}, u32[]{:S(2)}, u32[]{:S(2)}) collective-permute-start(bf16[192,768]{1,0:T(8,128)(2,1)S(1)} %collective-permute-done.8), channel_id=1, source_target_pairs={{1,0},{2,1},{3,2},{4,3},{5,4},{6,5},{7,6},{8,7},{9,8},{10,9},{11,1... | collective-permute-start | bytes 884744 | tf_op jit(solution)/shard_map/ppermute | solution.py:30
  31.2 8.9 %collective-permute-start.2 = (bf16[192,768]{1,0:T(8,128)(2,1)S(1)}, bf16[192,768]{1,0:T(8,128)(2,1)S(1)}, u32[]{:S(2)}, u32[]{:S(2)}) collective-permute-start(bf16[192,768]{1,0:T(8,128)(2,1)S(1)} %collective-permute-done.1), channel_id=1, source_target_pairs={{0,1},{1,2},{2,3},{3,4},{4,5},{5,6},{6,7},{7,8},{8,9},{9,10},{10,1... | collective-permute-start | bytes 884744 | tf_op jit(solution)/shard_map/ppermute | solution.py:27
  31.2 10.5 %collective-permute-start.10 = (bf16[192,768]{1,0:T(8,128)(2,1)S(1)}, bf16[192,768]{1,0:T(8,128)(2,1)S(1)}, u32[]{:S(2)}, u32[]{:S(2)}) collective-permute-start(bf16[192,768]{1,0:T(8,128)(2,1)S(1)} %collective-permute-done.9), channel_id=1, source_target_pairs={{1,0},{2,1},{3,2},{4,3},{5,4},{6,5},{7,6},{8,7},{9,8},{10,9},{11,1... | collective-permute-start | bytes 884744 | tf_op jit(solution)/shard_map/ppermute | solution.py:30
  40.2 9.5 %collective-permute-start.3 = (bf16[192,768]{1,0:T(8,128)(2,1)S(1)}, bf16[192,768]{1,0:T(8,128)(2,1)S(1)}, u32[]{:S(2)}, u32[]{:S(2)}) collective-permute-start(bf16[192,768]{1,0:T(8,128)(2,1)S(1)} %collective-permute-done.2), channel_id=1, source_target_pairs={{0,1},{1,2},{2,3},{3,4},{4,5},{5,6},{6,7},{7,8},{8,9},{9,10},{10,1... | collective-permute-start | bytes 884744 | tf_op jit(solution)/shard_map/ppermute | solution.py:27
  41.7 9.5 %collective-permute-start.11 = (bf16[192,768]{1,0:T(8,128)(2,1)S(1)}, bf16[192,768]{1,0:T(8,128)(2,1)S(1)}, u32[]{:S(2)}, u32[]{:S(2)}) collective-permute-start(bf16[192,768]{1,0:T(8,128)(2,1)S(1)} %collective-permute-done.10), channel_id=1, source_target_pairs={{1,0},{2,1},{3,2},{4,3},{5,4},{6,5},{7,6},{8,7},{9,8},{10,9},{11,1... | collective-permute-start | bytes 884744 | tf_op jit(solution)/shard_map/ppermute | solution.py:30
  49.7 96.8 %copy-start.16 = (bf16[192,768]{1,0:T(8,128)(2,1)}, bf16[192,768]{1,0:T(8,128)(2,1)S(1)}, u32[]{:S(2)}) copy-start(bf16[192,768]{1,0:T(8,128)(2,1)S(1)} %collective-permute-done.3) | copy-start | bytes 884740
  49.7 8.9 %collective-permute-start.4 = (bf16[192,768]{1,0:T(8,128)(2,1)S(1)}, bf16[192,768]{1,0:T(8,128)(2,1)S(1)}, u32[]{:S(2)}, u32[]{:S(2)}) collective-permute-start(bf16[192,768]{1,0:T(8,128)(2,1)S(1)} %collective-permute-done.3), channel_id=1, source_target_pairs={{0,1},{1,2},{2,3},{3,4},{4,5},{5,6},{6,7},{7,8},{8,9},{9,10},{10,1... | collective-permute-start | bytes 884744 | tf_op jit(solution)/shard_map/ppermute | solution.py:27
  51.2 82.5 %collective-permute-start.12 = (bf16[192,768]{1,0:T(8,128)(2,1)S(1)}, bf16[192,768]{1,0:T(8,128)(2,1)S(1)}, u32[]{:S(2)}, u32[]{:S(2)}) collective-permute-start(bf16[192,768]{1,0:T(8,128)(2,1)S(1)} %collective-permute-done.11), channel_id=1, source_target_pairs={{1,0},{2,1},{3,2},{4,3},{5,4},{6,5},{7,6},{8,7},{9,8},{10,9},{11,1... | collective-permute-start | bytes 884744 | tf_op jit(solution)/shard_map/ppermute | solution.py:30
  58.7 84.5 %copy-start.18 = (bf16[192,768]{1,0:T(8,128)(2,1)}, bf16[192,768]{1,0:T(8,128)(2,1)S(1)}, u32[]{:S(2)}) copy-start(bf16[192,768]{1,0:T(8,128)(2,1)S(1)} %collective-permute-done.4) | copy-start | bytes 884740
  58.7 75.1 %collective-permute-start.5 = (bf16[192,768]{1,0:T(8,128)(2,1)S(1)}, bf16[192,768]{1,0:T(8,128)(2,1)}, u32[]{:S(2)}, u32[]{:S(2)}) collective-permute-start(bf16[192,768]{1,0:T(8,128)(2,1)S(1)} %collective-permute-done.4), channel_id=1, source_target_pairs={{0,1},{1,2},{2,3},{3,4},{4,5},{5,6},{6,7},{7,8},{8,9},{9,10},{10,1... | collective-permute-start | bytes 884744 | tf_op jit(solution)/shard_map/ppermute | solution.py:27
  58.7 87.8 %copy-start.22 = (f32[128]{0:T(128)}, f32[128]{0:T(128)S(1)}, u32[]{:S(2)}) copy-start(f32[128]{0:T(128)S(1)} %broadcast_multiply_fusion.5) | copy-start | bytes 1540
  133.7 12.8 %copy-start.14 = (bf16[192,768]{1,0:T(8,128)(2,1)}, bf16[192,768]{1,0:T(8,128)(2,1)S(1)}, u32[]{:S(2)}) copy-start(bf16[192,768]{1,0:T(8,128)(2,1)S(1)} %collective-permute-done.12) | copy-start | bytes 884740
  133.7 4.4 collective-permute-start.13
  133.8 9.3 %collective-permute-start.6 = (bf16[192,768]{1,0:T(8,128)(2,1)}, bf16[192,768]{1,0:T(8,128)(2,1)}, u32[]{:S(2)}, u32[]{:S(2)}) collective-permute-start(bf16[192,768]{1,0:T(8,128)(2,1)} %collective-permute-done.5), channel_id=1, source_target_pairs={{0,1},{1,2},{2,3},{3,4},{4,5},{5,6},{6,7},{7,8},{8,9},{9,10},{10,1... | collective-permute-start | bytes 884744 | tf_op jit(solution)/shard_map/ppermute | solution.py:27
  138.1 37.2 %collective-permute-start.14 = (bf16[192,768]{1,0:T(8,128)(2,1)}, bf16[192,768]{1,0:T(8,128)(2,1)}, u32[]{:S(2)}, u32[]{:S(2)}) collective-permute-start(bf16[192,768]{1,0:T(8,128)(2,1)} %collective-permute-done.13), channel_id=1, source_target_pairs={{1,0},{2,1},{3,2},{4,3},{5,4},{6,5},{7,6},{8,7},{9,8},{10,9},{11,1... | collective-permute-start | bytes 884744 | tf_op jit(solution)/shard_map/ppermute | solution.py:30
  143.1 10.0 %collective-permute-start.7 = (bf16[192,768]{1,0:T(8,128)(2,1)}, bf16[192,768]{1,0:T(8,128)(2,1)}, u32[]{:S(2)}, u32[]{:S(2)}) collective-permute-start(bf16[192,768]{1,0:T(8,128)(2,1)} %collective-permute-done.6), channel_id=1, source_target_pairs={{0,1},{1,2},{2,3},{3,4},{4,5},{5,6},{6,7},{7,8},{8,9},{9,10},{10,1... | collective-permute-start | bytes 884744 | tf_op jit(solution)/shard_map/ppermute | solution.py:27
  149.6 18.7 %all-to-all-start = ((bf16[3,128,768]{1,0,2:T(4,128)(2,1)}), bf16[3,128,768]{1,0,2:T(4,128)(2,1)S(1)}, u32[]{:S(2)}, u32[]{:S(2)}) async-start(bf16[3,128,768]{1,0,2:T(4,128)(2,1)} %copy.66), calls=%async_computation | async-start | bytes 1572864 | tf_op jit(solution)/shard_map/all_to_all | solution.py:167
  171.7 10.9 %all-to-all-start.1 = ((bf16[2,128,384]{1,2,0:T(8,128)(2,1)}), bf16[2,128,384]{1,2,0:T(8,128)(2,1)S(1)}, u32[]{:S(2)}, u32[]{:S(2)}) async-start(bf16[2,128,384]{1,2,0:T(8,128)(2,1)} %copy.69), calls=%async_computation.1 | async-start | bytes 393216 | tf_op jit(solution)/shard_map/all_to_all | solution.py:175
  175.1 133.2 %reduce-scatter.25.cloned.1.call-start = ((), (), s32[]{:S(2)}) async-start(), calls=%async_computation.22 | async-start | bytes 2506752 | tf_op jit(solution)/shard_map/reduce_scatter | solution.py:279
  182.6 49.4 %copy-start.21 = (f32[3072]{0:T(1024)S(1)}, f32[3072]{0:T(1024)}, u32[]{:S(2)}) copy-start(f32[3072]{0:T(1024)} %convert_element_type.143) | copy-start | bytes 36868
  184.3 56.3 %copy-start.28 = (f32[128]{0:T(128)}, f32[128]{0:T(128)S(1)}, u32[]{:S(2)}) copy-start(f32[128]{0:T(128)S(1)} %broadcast_multiply_fusion.4) | copy-start | bytes 1540
  184.5 56.1 %copy-start.34 = (f32[128]{0:T(128)}, f32[128]{0:T(128)S(1)}, u32[]{:S(2)}) copy-start(f32[128]{0:T(128)S(1)} %add_rsqrt_fusion) | copy-start | bytes 1540
  184.6 50.8 %copy-start.6 = (f32[1,128,768]{2,1,0:T(8,128)S(1)}, f32[1,128,768]{2,1,0:T(8,128)}, u32[]{:S(2)}) copy-start(f32[1,128,768]{2,1,0:T(8,128)} %param.18) | copy-start | bytes 1179652
  246.4 127.9 %reduce-scatter.13.cloned.1.call-start = ((), (), s32[]{:S(2)}) async-start(), calls=%async_computation.16 | async-start | bytes 2506752 | tf_op jit(solution)/shard_map/reduce_scatter | solution.py:274
  290.0 150.4 %reduce-scatter.17.cloned.1.call-start = ((), (), s32[]{:S(2)}) async-start(), calls=%async_computation.18 | async-start | bytes 2506752 | tf_op jit(solution)/shard_map/reduce_scatter | solution.py:276
  292.3 214.1 %reduce-scatter.21.cloned.1.call-start = ((), (), s32[]{:S(2)}) async-start(), calls=%async_computation.20 | async-start | bytes 2506752 | tf_op jit(solution)/shard_map/reduce_scatter | solution.py:277
  294.6 326.0 %reduce-scatter.29.cloned.1.call-start = ((), (), s32[]{:S(2)}) async-start(), calls=%async_computation.24 | async-start | bytes 10027008 | tf_op jit(solution)/shard_map/reduce_scatter | solution.py:283
  300.9 436.6 %reduce-scatter.33.cloned.1.call-start = ((), (), s32[]{:S(2)}) async-start(), calls=%async_computation.26 | async-start | bytes 10027008 | tf_op jit(solution)/shard_map/reduce_scatter | solution.py:285
  307.4 67.0 %copy-start.37 = (bf16[768]{0:T(1024)(128)(2,1)S(1)}, bf16[768]{0:T(1024)(128)(2,1)}, u32[]{:S(2)}) copy-start(bf16[768]{0:T(1024)(128)(2,1)} %get-tuple-element.59) | copy-start | bytes 4612
  307.4 442.4 %reduce-scatter.27.cloned.1.call-start = ((), (), s32[]{:S(2)}) async-start(), calls=%async_computation.23 | async-start | bytes 221184 | tf_op jit(solution)/shard_map/reduce_scatter | solution.py:296
  308.3 454.2 %reduce-scatter.15.cloned.1.call-start = ((), (), s32[]{:S(2)}) async-start(), calls=%async_computation.17 | async-start | bytes 221184 | tf_op jit(solution)/shard_map/reduce_scatter | solution.py:291
  374.4 400.8 %reduce-scatter.19.cloned.1.call-start = ((), (), s32[]{:S(2)}) async-start(), calls=%async_computation.19 | async-start | bytes 221184 | tf_op jit(solution)/shard_map/reduce_scatter | solution.py:293
  440.4 347.4 %reduce-scatter.23.cloned.1.call-start = ((), (), s32[]{:S(2)}) async-start(), calls=%async_computation.21 | async-start | bytes 221184 | tf_op jit(solution)/shard_map/reduce_scatter | solution.py:294
  444.4 63.9 %copy-start.4 = (bf16[1,768,768]{2,1,0:T(8,128)(2,1)S(1)}, bf16[1,768,768]{2,1,0:T(8,128)(2,1)}, u32[]{:S(2)}) copy-start(bf16[1,768,768]{2,1,0:T(8,128)(2,1)} %all-gather.22.cloned.1.call-done) | copy-start | bytes 3538948
  506.4 298.9 %reduce-scatter.31.cloned.1.call-start = ((), (), s32[]{:S(2)}) async-start(), calls=%async_computation.25 | async-start | bytes 884736 | tf_op jit(solution)/shard_map/reduce_scatter | solution.py:300
  508.3 113.5 %copy-start.3 = (bf16[1,768,768]{2,1,0:T(8,128)(2,1)S(1)}, bf16[1,768,768]{2,1,0:T(8,128)(2,1)}, u32[]{:S(2)}) copy-start(bf16[1,768,768]{2,1,0:T(8,128)(2,1)} %all-gather.24.cloned.1.call-done) | copy-start | bytes 3538948
  508.3 113.5 %copy-start.24 = (f32[128]{0:T(128)S(1)}, f32[128]{0:T(128)}, u32[]{:S(2)}) copy-start(f32[128]{0:T(128)} %copy-done.22) | copy-start | bytes 1540
  508.3 113.5 %copy-start.27 = (f32[128]{0:T(128)S(1)}, f32[128]{0:T(128)}, u32[]{:S(2)}) copy-start(f32[128]{0:T(128)} %copy-done.25) | copy-start | bytes 1540
  620.7 202.1 %reduce-scatter.35.cloned.1.call-start = ((), (), s32[]{:S(2)}) async-start(), calls=%async_computation.27 | async-start | bytes 884736 | tf_op jit(solution)/shard_map/reduce_scatter | solution.py:302
  (26 other events, 86.7 us)
Sparse Core Ops, SparseCore 0:
  10.3 44.9 all-gather.23
  57.5 37.3 all-gather.19
  97.2 39.5 all-gather.21
  138.9 38.8 all-gather.25
  180.0 51.9 all-gather.27
  246.5 61.7 reduce-scatter.24
  312.1 62.2 reduce-scatter.12
  378.1 62.2 reduce-scatter.16
  444.1 62.2 reduce-scatter.20
  510.3 110.2 reduce-scatter.28
  624.7 112.7 reduce-scatter.32
  739.6 10.1 reduce-scatter.26
  752.0 10.5 reduce-scatter.14
  764.6 10.5 reduce-scatter.18
  777.2 10.5 reduce-scatter.22
  789.9 15.3 reduce-scatter.30
  807.4 15.3 reduce-scatter.34
